TPU v7x, 32 devices: a whole 2x2x4 slice. The times are simulated.
32 devices in a mesh: outer: 4 (over y, x), inner: 8 (over z, core).
Axes of the slice: x: 2, y: 2, z: 4, core: 2. Of those that a mesh axis runs over, the one named last changes fastest.
Arguments:
- queries: bfloat16 [4096, 4096], P(('outer', 'inner')), may hold values from -24 to 24, as said below
- keys: bfloat16 [4096, 1024], P(('outer', 'inner')), may hold values from -24 to 24, as said below
- values: bfloat16 [4096, 1024], P(('outer', 'inner')), may hold values from -6 to 6
Outputs:
- attended: bfloat16 [4096, 4096], P(('outer', 'inner'))
Inputs may be any that keep to these rules, and one draw needn't show every extreme that they name: `queries`: entries of order one, a few larger. `keys`: entries of order one, a few larger.
All inputs are finite; a program needn't handle non-finite values.
Results may differ from a plain program's by a relative error of at most 0.008.
Values may be sent and summed in bfloat16 or wider, within the bound.
No kernel may reach another device: no remote copies, remote signals or barrier semaphores. Data moves between devices by JAX's collectives and lax.ppermute only.
A program may use at most 128 MiB of HBM per device.

v0:
```python
import jax
import jax.numpy as jnp
from jax import lax
from jax.sharding import PartitionSpec as P

QH = 32
KVH = 8
HD = 128


def shifted(block, axis, distance):
    devices = range(lax.axis_size(axis))
    route = [(i - distance, i) for i in devices if i - distance in devices]
    return lax.ppermute(block, axis, route)


def attend(state, near_keys, near_values, allowed, grouped):
    rows = near_keys.shape[0]
    heads = near_keys.shape[1]
    size = 256
    count = rows // size
    scale = 1.0 / HD**0.5
    key_blocks = near_keys.reshape(count, size, heads, HD)
    value_blocks = near_values.reshape(count, size, heads, HD)

    def one_block(carry, pieces):
        peak, total, accum = carry
        key_block, value_block = pieces
        scores = (
            jnp.einsum("qgrd,kgd->grqk", grouped, key_block, preferred_element_type=jnp.float32)
            * scale
        )
        scores = jnp.where(allowed, scores, -jnp.inf)
        upper = jnp.maximum(peak, jnp.max(scores, axis=-1))
        factor = jnp.exp(peak - upper)
        weights = jnp.exp(scores - upper[..., None])
        total = total * factor + jnp.sum(weights, axis=-1)
        update = jnp.einsum(
            "grqk,kgd->grqd",
            weights.astype(jnp.bfloat16),
            value_block,
            preferred_element_type=jnp.float32,
        )
        accum = accum * factor[..., None] + update
        return ((upper, total, accum), None)

    state, unused = lax.scan(one_block, state, (key_blocks, value_blocks))
    return state


def fresh_state(heads, ratio, tokens):
    return (
        jnp.full((heads, ratio, tokens), -jnp.inf, jnp.float32),
        jnp.zeros((heads, ratio, tokens), jnp.float32),
        jnp.zeros((heads, ratio, tokens, HD), jnp.float32),
    )


def shards(queries, keys, values):
    tokens = queries.shape[0]
    position = lax.axis_index("outer")
    before_ok = position > 0
    after_ok = position < lax.axis_size("outer") - 1
    members = lax.axis_size("inner")
    per_device = QH // members
    repeat = members // KVH
    query_heads = queries.reshape(tokens, QH, HD)
    key_heads = jnp.repeat(keys.reshape(tokens, KVH, HD), repeat, axis=1)
    value_heads = jnp.repeat(values.reshape(tokens, KVH, HD), repeat, axis=1)
    group_q, group_k, group_v = (
        lax.all_to_all(query_heads, "inner", split_axis=1, concat_axis=0, tiled=True),
        lax.all_to_all(key_heads, "inner", split_axis=1, concat_axis=0, tiled=True),
        lax.all_to_all(value_heads, "inner", split_axis=1, concat_axis=0, tiled=True),
    )
    rows = group_q.shape[0]
    grouped = group_q.reshape(rows, 1, per_device, HD)
    state = attend(fresh_state(1, per_device, rows), group_k, group_v, True, grouped)
    early_k, early_v = shifted((group_k, group_v), "outer", 1)
    state = attend(state, early_k, early_v, before_ok, grouped)
    late_k, late_v = shifted((group_k, group_v), "outer", -1)
    state = attend(state, late_k, late_v, after_ok, grouped)
    peak, total, accum = state
    mixed = (accum / total[..., None]).astype(jnp.bfloat16)
    mixed = mixed.reshape(per_device, rows, HD).transpose(1, 0, 2)
    back = lax.all_to_all(mixed, "inner", split_axis=0, concat_axis=1, tiled=True)
    return back.reshape(tokens, QH * HD)


def solution(mesh):
    placed = (P(("outer", "inner"), None), P(("outer", "inner"), None), P(("outer", "inner"), None))
    return jax.shard_map(
        shards, mesh=mesh, in_specs=placed, out_specs=P(("outer", "inner"), None), check_vma=False
    )
```

profile of v0, /device:TPU:0, one launch (start us, length us, event | category | flops | bytes accessed | tf_op | source)
XLA Modules:
  0.0 174.7 jit_solution(10812905736298252282)
XLA Ops:
  0.0 0.9 copy-done
  1.0 0.8 copy_bitcast_fusion.1
  1.7 6.4 %all-to-all-start = ((bf16[128,8,128]{2,0,1:T(8,128)(2,1)}), bf16[128,8,128]{2,0,1:T(8,128)(2,1)S(1)}, u32[]{:S(2)}, u32[]{:S(2)}) async-start(bf16[128,8,128]{2,0,1:T(8,128)(2,1)} %copy_bitcast_fusion.1), calls=%async_computation | async-start | bytes 524288 | tf_op jit(solution)/shard_map/all_to_all | solution.py:72
  8.1 1.7 copy_bitcast_fusion
  9.8 8.0 %all-to-all-done = bf16[128,8,128]{2,0,1:T(8,128)(2,1)S(1)} async-done(((bf16[128,8,128]{2,0,1:T(8,128)(2,1)}), bf16[128,8,128]{2,0,1:T(8,128)(2,1)S(1)}, u32[]{:S(2)}, u32[]{:S(2)}) %all-to-all-start) | async-done | bytes 262176 | tf_op jit(solution)/shard_map/all_to_all | solution.py:72
  17.8 3.4 %all-to-all-start.2 = ((bf16[128,8,128]{2,0,1:T(8,128)(2,1)}), bf16[128,8,128]{2,0,1:T(8,128)(2,1)S(1)}, u32[]{:S(2)}, u32[]{:S(2)}) async-start(bf16[128,8,128]{2,0,1:T(8,128)(2,1)} %copy_bitcast_fusion), calls=%async_computation.2 | async-start | bytes 524288 | tf_op jit(solution)/shard_map/all_to_all | solution.py:73
  21.2 2.3 %copy.29 = bf16[128,4096]{0,1:T(8,128)(2,1)} copy(bf16[128,4096]{1,0:T(8,128)(2,1)} %param.9) | data formatting | bytes 2097152 | tf_op args[0]
  23.5 7.4 %all-to-all-done.2 = bf16[128,8,128]{2,0,1:T(8,128)(2,1)S(1)} async-done(((bf16[128,8,128]{2,0,1:T(8,128)(2,1)}), bf16[128,8,128]{2,0,1:T(8,128)(2,1)S(1)}, u32[]{:S(2)}, u32[]{:S(2)}) %all-to-all-start.2) | async-done | bytes 262176 | tf_op jit(solution)/shard_map/all_to_all | solution.py:73
  30.8 0.7 copy-done.4
  31.5 3.6 %all-to-all-start.1 = ((bf16[128,32,128]{0,2,1:T(8,128)(2,1)}), bf16[128,32,128]{0,2,1:T(8,128)(2,1)S(1)}, u32[]{:S(2)}, u32[]{:S(2)}) async-start(bf16[128,32,128]{0,2,1:T(8,128)(2,1)} %bitcast.31), calls=%async_computation.1 | async-start | bytes 2097152 | tf_op jit(solution)/shard_map/all_to_all | solution.py:71
  35.1 4.1 %collective-permute-start = (bf16[1024,1,128]{2,0,1:T(8,128)(2,1)}, bf16[1024,1,128]{2,0,1:T(8,128)(2,1)}, u32[]{:S(2)}, u32[]{:S(2)}) collective-permute-start(bf16[1024,1,128]{2,0,1:T(8,128)(2,1)} %bitcast.261), channel_id=1, source_target_pairs={{0,8},{8,16},{16,24},{1,9},{9,17},{17,25},{2,10},{10,18},{18,26},{... | collective-permute-start | bytes 786440 | tf_op jit(solution)/shard_map/ppermute | solution.py:14
  39.3 1.3 collective-permute-start.2
  40.5 5.3 %collective-permute-start.1 = (bf16[1024,1,128]{2,0,1:T(8,128)(2,1)}, bf16[1024,1,128]{2,0,1:T(8,128)(2,1)}, u32[]{:S(2)}, u32[]{:S(2)}) collective-permute-start(bf16[1024,1,128]{2,0,1:T(8,128)(2,1)} %bitcast.264), channel_id=1, source_target_pairs={{0,8},{8,16},{16,24},{1,9},{9,17},{17,25},{2,10},{10,18},{18,26},{... | collective-permute-start | bytes 786440 | tf_op jit(solution)/shard_map/ppermute | solution.py:14
  45.8 1.3 collective-permute-start.3
  47.1 14.5 %all-to-all-done.1 = bf16[128,32,128]{0,2,1:T(8,128)(2,1)S(1)} async-done(((bf16[128,32,128]{0,2,1:T(8,128)(2,1)}), bf16[128,32,128]{0,2,1:T(8,128)(2,1)S(1)}, u32[]{:S(2)}, u32[]{:S(2)}) %all-to-all-start.1) | async-done | bytes 1048608 | tf_op jit(solution)/shard_map/all_to_all | solution.py:71
  61.6 1.0 copy-done.2
  62.6 1.6 copy.31
  64.2 31.1 %while.45 = (s32[]{:T(128)}, f32[1,4,1024]{2,1,0:T(4,128)S(1)}, f32[1,4,1024]{2,1,0:T(4,128)S(1)}, f32[1,4,1024,128]{3,2,1,0:T(8,128)S(1)}, bf16[4,256,1,128]{3,...) while((s32[]{:T(128)}, f32[1,4,1024]{2,1,0:T(4,128)S(1)}, ...), condition=%wide.region_3.4_spmd.clone, body=%wide.region_0.3_spmd.clone.sunk | while | flops 546856960 | bytes 34997380 | solution.py:47
  64.2 3.5 %bitcast_reduce_fusion.8 = (f32[4,1024]{1,0:T(4,128)S(1)}, f32[256,1024,4]{1,0,2:T(8,128)}) fusion(bf16[1024,1,4,128]{3,0,2,1:T(8,128)(2,1)S(1)} %get-tuple-element.409, bf16[4,256,1,128]{3,1,2,0:T(8,128)(2,1)} %get-tuple-element.408, s32[]{:T(128)} %get-tuple-element.395), kind=kOutput, calls=%fused_computation.55.clone.1 | convolution fusion | flops 270528512 | bytes 5325312 | tf_op jit(solution)/shard_map/while/body/eval_jaxpr/qgrd,kgd->grqk/dot_general | solution.py:30
  67.7 3.3 %bitcast_add_fusion.17 = f32[1,4,1024,128]{3,2,1,0:T(8,128)S(1)} fusion(f32[1,4,1024,128]{3,2,1,0:T(8,128)S(1)} %get-tuple-element.398, f32[256,1024,4]{1,0,2:T(8,128)} %get-tuple-element.384, f32[4,1024]{1,0:T(4,128)S(1)} %bitcast.252, f32[4,1024]{1,0:T(4,128)S(1)} %get-tuple-element.385, pred[]{:T(512)S(6)} %compare.3, ...), kind=kOutput, calls=%fused_computation.61.clone.1 | convolution fusion | flops 273154048 | bytes 8487425 | tf_op jit(solution)/shard_map/while/body/eval_jaxpr/grqk,kgd->grqd/dot_general | solution.py:38
  71.2 0.7 fusion.93
  72.0 3.5 %bitcast_reduce_fusion.8 = (f32[4,1024]{1,0:T(4,128)S(1)}, f32[256,1024,4]{1,0,2:T(8,128)}) fusion(bf16[1024,1,4,128]{3,0,2,1:T(8,128)(2,1)S(1)} %get-tuple-element.409, bf16[4,256,1,128]{3,1,2,0:T(8,128)(2,1)} %get-tuple-element.408, s32[]{:T(128)} %get-tuple-element.395), kind=kOutput, calls=%fused_computation.55.clone.1 | convolution fusion | flops 270528512 | bytes 5325312 | tf_op jit(solution)/shard_map/while/body/eval_jaxpr/qgrd,kgd->grqk/dot_general | solution.py:30
  75.5 3.3 %bitcast_add_fusion.17 = f32[1,4,1024,128]{3,2,1,0:T(8,128)S(1)} fusion(f32[1,4,1024,128]{3,2,1,0:T(8,128)S(1)} %get-tuple-element.398, f32[256,1024,4]{1,0,2:T(8,128)} %get-tuple-element.384, f32[4,1024]{1,0:T(4,128)S(1)} %bitcast.252, f32[4,1024]{1,0:T(4,128)S(1)} %get-tuple-element.385, pred[]{:T(512)S(6)} %compare.3, ...), kind=kOutput, calls=%fused_computation.61.clone.1 | convolution fusion | flops 273154048 | bytes 8487425 | tf_op jit(solution)/shard_map/while/body/eval_jaxpr/grqk,kgd->grqd/dot_general | solution.py:38
  78.8 0.2 copy-done.1
  79.0 0.7 fusion.93
  79.7 3.5 %bitcast_reduce_fusion.8 = (f32[4,1024]{1,0:T(4,128)S(1)}, f32[256,1024,4]{1,0,2:T(8,128)}) fusion(bf16[1024,1,4,128]{3,0,2,1:T(8,128)(2,1)S(1)} %get-tuple-element.409, bf16[4,256,1,128]{3,1,2,0:T(8,128)(2,1)} %get-tuple-element.408, s32[]{:T(128)} %get-tuple-element.395), kind=kOutput, calls=%fused_computation.55.clone.1 | convolution fusion | flops 270528512 | bytes 5325312 | tf_op jit(solution)/shard_map/while/body/eval_jaxpr/qgrd,kgd->grqk/dot_general | solution.py:30
  83.3 3.3 %bitcast_add_fusion.17 = f32[1,4,1024,128]{3,2,1,0:T(8,128)S(1)} fusion(f32[1,4,1024,128]{3,2,1,0:T(8,128)S(1)} %get-tuple-element.398, f32[256,1024,4]{1,0,2:T(8,128)} %get-tuple-element.384, f32[4,1024]{1,0:T(4,128)S(1)} %bitcast.252, f32[4,1024]{1,0:T(4,128)S(1)} %get-tuple-element.385, pred[]{:T(512)S(6)} %compare.3, ...), kind=kOutput, calls=%fused_computation.61.clone.1 | convolution fusion | flops 273154048 | bytes 8487425 | tf_op jit(solution)/shard_map/while/body/eval_jaxpr/grqk,kgd->grqd/dot_general | solution.py:38
  86.6 0.2 copy-done.1
  86.7 0.7 fusion.93
  87.5 3.5 %bitcast_reduce_fusion.8 = (f32[4,1024]{1,0:T(4,128)S(1)}, f32[256,1024,4]{1,0,2:T(8,128)}) fusion(bf16[1024,1,4,128]{3,0,2,1:T(8,128)(2,1)S(1)} %get-tuple-element.409, bf16[4,256,1,128]{3,1,2,0:T(8,128)(2,1)} %get-tuple-element.408, s32[]{:T(128)} %get-tuple-element.395), kind=kOutput, calls=%fused_computation.55.clone.1 | convolution fusion | flops 270528512 | bytes 5325312 | tf_op jit(solution)/shard_map/while/body/eval_jaxpr/qgrd,kgd->grqk/dot_general | solution.py:30
  91.0 3.3 %bitcast_add_fusion.17 = f32[1,4,1024,128]{3,2,1,0:T(8,128)S(1)} fusion(f32[1,4,1024,128]{3,2,1,0:T(8,128)S(1)} %get-tuple-element.398, f32[256,1024,4]{1,0,2:T(8,128)} %get-tuple-element.384, f32[4,1024]{1,0:T(4,128)S(1)} %bitcast.252, f32[4,1024]{1,0:T(4,128)S(1)} %get-tuple-element.385, pred[]{:T(512)S(6)} %compare.3, ...), kind=kOutput, calls=%fused_computation.61.clone.1 | convolution fusion | flops 273154048 | bytes 8487425 | tf_op jit(solution)/shard_map/while/body/eval_jaxpr/grqk,kgd->grqd/dot_general | solution.py:38
  94.3 0.2 copy-done.1
  94.5 0.7 fusion.93
  95.3 20.8 %while.43 = (s32[]{:T(128)}, f32[1,4,1024]{2,1,0:T(4,128)S(1)}, f32[1,4,1024]{2,1,0:T(4,128)S(1)}, f32[1,4,1024,128]{3,2,1,0:T(8,128)S(1)}, pred[]{:T(512)}, /*i...) while((s32[]{:T(128)}, f32[1,4,1024]{2,1,0:T(4,128)S(1)}, ...), condition=%wide.region_7.8_spmd, body=%wide.region_4.7_spmd.sunk | while | flops 549466112 | bytes 18221148 | solution.py:47
  95.3 1.6 bitcast_reduce_fusion.6
  96.9 2.7 %bitcast_add_fusion.13 = f32[1,4,1024,128]{3,2,1,0:T(8,128)S(1)} fusion(f32[1,4,1024,128]{3,2,1,0:T(8,128)S(1)} %get-tuple-element.425, f32[256,1024,4]{1,0,2:T(8,128)S(1)} %get-tuple-element.361, f32[4,1024]{1,0:T(4,128)S(1)} %bitcast.254, pred[]{:T(512)} %get-tuple-element.435, f32[4,1024]{1,0:T(4,128)S(1)} %get-tuple-element.362, ...), kind=kOutput, calls=%fused_computation.8.clone.1 | convolution fusion | flops 273678336 | bytes 8487936 | tf_op jit(solution)/shard_map/while/body/eval_jaxpr/grqk,kgd->grqd/dot_general | solution.py:38
  99.6 0.9 fusion.85
  100.5 1.6 bitcast_reduce_fusion.6
  102.1 2.7 %bitcast_add_fusion.13 = f32[1,4,1024,128]{3,2,1,0:T(8,128)S(1)} fusion(f32[1,4,1024,128]{3,2,1,0:T(8,128)S(1)} %get-tuple-element.425, f32[256,1024,4]{1,0,2:T(8,128)S(1)} %get-tuple-element.361, f32[4,1024]{1,0:T(4,128)S(1)} %bitcast.254, pred[]{:T(512)} %get-tuple-element.435, f32[4,1024]{1,0:T(4,128)S(1)} %get-tuple-element.362, ...), kind=kOutput, calls=%fused_computation.8.clone.1 | convolution fusion | flops 273678336 | bytes 8487936 | tf_op jit(solution)/shard_map/while/body/eval_jaxpr/grqk,kgd->grqd/dot_general | solution.py:38
  104.8 0.9 fusion.85
  105.7 1.6 bitcast_reduce_fusion.6
  107.3 2.7 %bitcast_add_fusion.13 = f32[1,4,1024,128]{3,2,1,0:T(8,128)S(1)} fusion(f32[1,4,1024,128]{3,2,1,0:T(8,128)S(1)} %get-tuple-element.425, f32[256,1024,4]{1,0,2:T(8,128)S(1)} %get-tuple-element.361, f32[4,1024]{1,0:T(4,128)S(1)} %bitcast.254, pred[]{:T(512)} %get-tuple-element.435, f32[4,1024]{1,0:T(4,128)S(1)} %get-tuple-element.362, ...), kind=kOutput, calls=%fused_computation.8.clone.1 | convolution fusion | flops 273678336 | bytes 8487936 | tf_op jit(solution)/shard_map/while/body/eval_jaxpr/grqk,kgd->grqd/dot_general | solution.py:38
  110.0 0.9 fusion.85
  110.9 1.6 bitcast_reduce_fusion.6
  112.5 2.7 %bitcast_add_fusion.13 = f32[1,4,1024,128]{3,2,1,0:T(8,128)S(1)} fusion(f32[1,4,1024,128]{3,2,1,0:T(8,128)S(1)} %get-tuple-element.425, f32[256,1024,4]{1,0,2:T(8,128)S(1)} %get-tuple-element.361, f32[4,1024]{1,0:T(4,128)S(1)} %bitcast.254, pred[]{:T(512)} %get-tuple-element.435, f32[4,1024]{1,0:T(4,128)S(1)} %get-tuple-element.362, ...), kind=kOutput, calls=%fused_computation.8.clone.1 | convolution fusion | flops 273678336 | bytes 8487936 | tf_op jit(solution)/shard_map/while/body/eval_jaxpr/grqk,kgd->grqd/dot_general | solution.py:38
  115.2 0.9 fusion.85
  116.1 20.8 %while.44 = (s32[]{:T(128)}, f32[1,4,1024]{2,1,0:T(4,128)S(1)}, f32[1,4,1024]{2,1,0:T(4,128)S(1)}, f32[1,4,1024,128]{3,2,1,0:T(8,128)S(1)}, pred[]{:T(512)}, /*i...) while((s32[]{:T(128)}, f32[1,4,1024]{2,1,0:T(4,128)S(1)}, ...), condition=%wide.region_11.12_spmd, body=%wide.region_8.11_spmd.sunk | while | flops 549466112 | bytes 18221148 | solution.py:47
  116.1 1.6 bitcast_reduce_fusion.7
  117.7 2.7 %bitcast_add_fusion.15 = f32[1,4,1024,128]{3,2,1,0:T(8,128)S(1)} fusion(f32[1,4,1024,128]{3,2,1,0:T(8,128)S(1)} %get-tuple-element.452, f32[256,1024,4]{1,0,2:T(8,128)S(1)} %get-tuple-element.373, f32[4,1024]{1,0:T(4,128)S(1)} %bitcast.256, pred[]{:T(512)} %get-tuple-element.462, f32[4,1024]{1,0:T(4,128)S(1)} %get-tuple-element.374, ...), kind=kOutput, calls=%fused_computation.35.clone.1 | convolution fusion | flops 273678336 | bytes 8487936 | tf_op jit(solution)/shard_map/while/body/eval_jaxpr/grqk,kgd->grqd/dot_general | solution.py:38
  120.4 0.9 fusion.89
  121.3 1.6 bitcast_reduce_fusion.7
  122.9 2.7 %bitcast_add_fusion.15 = f32[1,4,1024,128]{3,2,1,0:T(8,128)S(1)} fusion(f32[1,4,1024,128]{3,2,1,0:T(8,128)S(1)} %get-tuple-element.452, f32[256,1024,4]{1,0,2:T(8,128)S(1)} %get-tuple-element.373, f32[4,1024]{1,0:T(4,128)S(1)} %bitcast.256, pred[]{:T(512)} %get-tuple-element.462, f32[4,1024]{1,0:T(4,128)S(1)} %get-tuple-element.374, ...), kind=kOutput, calls=%fused_computation.35.clone.1 | convolution fusion | flops 273678336 | bytes 8487936 | tf_op jit(solution)/shard_map/while/body/eval_jaxpr/grqk,kgd->grqd/dot_general | solution.py:38
  125.6 0.9 fusion.89
  126.5 1.6 bitcast_reduce_fusion.7
  128.1 2.7 %bitcast_add_fusion.15 = f32[1,4,1024,128]{3,2,1,0:T(8,128)S(1)} fusion(f32[1,4,1024,128]{3,2,1,0:T(8,128)S(1)} %get-tuple-element.452, f32[256,1024,4]{1,0,2:T(8,128)S(1)} %get-tuple-element.373, f32[4,1024]{1,0:T(4,128)S(1)} %bitcast.256, pred[]{:T(512)} %get-tuple-element.462, f32[4,1024]{1,0:T(4,128)S(1)} %get-tuple-element.374, ...), kind=kOutput, calls=%fused_computation.35.clone.1 | convolution fusion | flops 273678336 | bytes 8487936 | tf_op jit(solution)/shard_map/while/body/eval_jaxpr/grqk,kgd->grqd/dot_general | solution.py:38
  130.8 0.9 fusion.89
  131.7 1.6 bitcast_reduce_fusion.7
  133.3 2.7 %bitcast_add_fusion.15 = f32[1,4,1024,128]{3,2,1,0:T(8,128)S(1)} fusion(f32[1,4,1024,128]{3,2,1,0:T(8,128)S(1)} %get-tuple-element.452, f32[256,1024,4]{1,0,2:T(8,128)S(1)} %get-tuple-element.373, f32[4,1024]{1,0:T(4,128)S(1)} %bitcast.256, pred[]{:T(512)} %get-tuple-element.462, f32[4,1024]{1,0:T(4,128)S(1)} %get-tuple-element.374, ...), kind=kOutput, calls=%fused_computation.35.clone.1 | convolution fusion | flops 273678336 | bytes 8487936 | tf_op jit(solution)/shard_map/while/body/eval_jaxpr/grqk,kgd->grqd/dot_general | solution.py:38
  136.0 0.9 fusion.89
  136.9 0.2 copy.33
  137.2 6.5 %fusion.67 = bf16[1024,4,128]{2,1,0:T(4,128)(2,1)S(1)} fusion(f32[4,1024]{0,1:T(8,128)S(1)} %copy.33, f32[1,4,1024,128]{3,2,1,0:T(8,128)S(1)} %get-tuple-element.137), kind=kLoop, calls=%fused_computation.81 | loop fusion | flops 1048576 | bytes 3162112 | tf_op jit(solution)/shard_map/transpose | solution.py:84
  143.7 29.0 %all_to_all.66 = bf16[1024,4,128]{2,1,0:T(4,128)(2,1)S(1)} all-to-all(bf16[1024,4,128]{2,1,0:T(4,128)(2,1)S(1)} %fusion.67), channel_id=1, replica_groups=mesh['outer'=4,'inner'=8] {'inner'}, dimensions={0} | all-to-all | bytes 2097152 | tf_op jit(solution)/shard_map/all_to_all | solution.py:85
  172.7 0.4 copy.35
  173.1 1.6 reshape.130
  (53 shorter events, 0.7 us)
Async XLA Ops:
  0.0 1.0 copy-start
  1.7 16.1 %all-to-all-start = ((bf16[128,8,128]{2,0,1:T(8,128)(2,1)}), bf16[128,8,128]{2,0,1:T(8,128)(2,1)S(1)}, u32[]{:S(2)}, u32[]{:S(2)}) async-start(bf16[128,8,128]{2,0,1:T(8,128)(2,1)} %copy_bitcast_fusion.1), calls=%async_computation | async-start | bytes 524288 | tf_op jit(solution)/shard_map/all_to_all | solution.py:72
  17.8 13.1 %copy-start.3 = (bf16[128,8,128]{2,0,1:T(8,128)(2,1)}, bf16[128,8,128]{2,0,1:T(8,128)(2,1)S(1)}, u32[]{:S(2)}) copy-start(bf16[128,8,128]{2,0,1:T(8,128)(2,1)S(1)} %all-to-all-done) | copy-start | bytes 786436
  17.8 13.1 %all-to-all-start.2 = ((bf16[128,8,128]{2,0,1:T(8,128)(2,1)}), bf16[128,8,128]{2,0,1:T(8,128)(2,1)S(1)}, u32[]{:S(2)}, u32[]{:S(2)}) async-start(bf16[128,8,128]{2,0,1:T(8,128)(2,1)} %copy_bitcast_fusion), calls=%async_computation.2 | async-start | bytes 524288 | tf_op jit(solution)/shard_map/all_to_all | solution.py:73
  30.8 0.7 copy-start.4
  31.5 30.1 %all-to-all-start.1 = ((bf16[128,32,128]{0,2,1:T(8,128)(2,1)}), bf16[128,32,128]{0,2,1:T(8,128)(2,1)S(1)}, u32[]{:S(2)}, u32[]{:S(2)}) async-start(bf16[128,32,128]{0,2,1:T(8,128)(2,1)} %bitcast.31), calls=%async_computation.1 | async-start | bytes 2097152 | tf_op jit(solution)/shard_map/all_to_all | solution.py:71
  35.1 60.1 %collective-permute-start = (bf16[1024,1,128]{2,0,1:T(8,128)(2,1)}, bf16[1024,1,128]{2,0,1:T(8,128)(2,1)}, u32[]{:S(2)}, u32[]{:S(2)}) collective-permute-start(bf16[1024,1,128]{2,0,1:T(8,128)(2,1)} %bitcast.261), channel_id=1, source_target_pairs={{0,8},{8,16},{16,24},{1,9},{9,17},{17,25},{2,10},{10,18},{18,26},{... | collective-permute-start | bytes 786440 | tf_op jit(solution)/shard_map/ppermute | solution.py:14
  39.3 76.8 %collective-permute-start.2 = (bf16[1024,1,128]{2,0,1:T(8,128)(2,1)}, bf16[1024,1,128]{2,0,1:T(8,128)(2,1)}, u32[]{:S(2)}, u32[]{:S(2)}) collective-permute-start(bf16[1024,1,128]{2,0,1:T(8,128)(2,1)} %bitcast.262), channel_id=1, source_target_pairs={{8,0},{16,8},{24,16},{9,1},{17,9},{25,17},{10,2},{18,10},{26,18},{... | collective-permute-start | bytes 786440 | tf_op jit(solution)/shard_map/ppermute | solution.py:14
  40.5 54.7 %collective-permute-start.1 = (bf16[1024,1,128]{2,0,1:T(8,128)(2,1)}, bf16[1024,1,128]{2,0,1:T(8,128)(2,1)}, u32[]{:S(2)}, u32[]{:S(2)}) collective-permute-start(bf16[1024,1,128]{2,0,1:T(8,128)(2,1)} %bitcast.264), channel_id=1, source_target_pairs={{0,8},{8,16},{16,24},{1,9},{9,17},{17,25},{2,10},{10,18},{18,26},{... | collective-permute-start | bytes 786440 | tf_op jit(solution)/shard_map/ppermute | solution.py:14
  45.8 70.3 %collective-permute-start.3 = (bf16[1024,1,128]{2,0,1:T(8,128)(2,1)}, bf16[1024,1,128]{2,0,1:T(8,128)(2,1)}, u32[]{:S(2)}, u32[]{:S(2)}) collective-permute-start(bf16[1024,1,128]{2,0,1:T(8,128)(2,1)} %bitcast.265), channel_id=1, source_target_pairs={{8,0},{16,8},{24,16},{9,1},{17,9},{25,17},{10,2},{18,10},{26,18},{... | collective-permute-start | bytes 786440 | tf_op jit(solution)/shard_map/ppermute | solution.py:14
  61.6 1.0 copy-start.2
  67.7 3.5 %copy-start.1 = (f32[256,1024,4]{1,0,2:T(8,128)S(1)}, f32[256,1024,4]{1,0,2:T(8,128)}, u32[]{:S(2)}) copy-start(f32[256,1024,4]{1,0,2:T(8,128)} %get-tuple-element.384) | copy-start | bytes 12582916 | tf_op jit(solution)/shard_map/while
  75.5 3.5 %copy-start.1 = (f32[256,1024,4]{1,0,2:T(8,128)S(1)}, f32[256,1024,4]{1,0,2:T(8,128)}, u32[]{:S(2)}) copy-start(f32[256,1024,4]{1,0,2:T(8,128)} %get-tuple-element.384) | copy-start | bytes 12582916 | tf_op jit(solution)/shard_map/while
  83.3 3.5 %copy-start.1 = (f32[256,1024,4]{1,0,2:T(8,128)S(1)}, f32[256,1024,4]{1,0,2:T(8,128)}, u32[]{:S(2)}) copy-start(f32[256,1024,4]{1,0,2:T(8,128)} %get-tuple-element.384) | copy-start | bytes 12582916 | tf_op jit(solution)/shard_map/while
  91.0 3.5 %copy-start.1 = (f32[256,1024,4]{1,0,2:T(8,128)S(1)}, f32[256,1024,4]{1,0,2:T(8,128)}, u32[]{:S(2)}) copy-start(f32[256,1024,4]{1,0,2:T(8,128)} %get-tuple-element.384) | copy-start | bytes 12582916 | tf_op jit(solution)/shard_map/while
where the time goes:
time: 176 us; the launch traced here: 175 us
  matrix products  61.1 us (35%)
  waiting for transfers between devices  29.9 us (17%)
  blocking collectives  29 us (16%)
  starting transfers between devices  25.3 us (14%)
  other arithmetic  16.8 us (10%)
  local copies, waits for them, and re-layouts  11.9 us (7%)
    dot_general x12, matrix products, one_block(): jnp.einsum('grqk,kgd->grqd', weights.astype(jnp.bfloat16), value_block, p...  34.6 us
    all_to_all x1, blocking collectives, shards(): lax.all_to_all(mixed, 'inner', split_axis=0, concat_axis=1, tiled=True)  29 us
    dot_general x12, matrix products, one_block(): jnp.einsum('qgrd,kgd->grqk', grouped, key_block, preferred_element_type=j...  26.5 us
    all_to_all x1, waiting for transfers between devices, shards(): lax.all_to_all(query_heads, 'inner', split_axis=1, concat_axis=0, tiled=T...  14.5 us
    ppermute x4, starting transfers between devices, shifted(): return lax.ppermute(block, axis, route)  11.9 us
    reduce_sum x12, other arithmetic, one_block(): total = total * factor + jnp.sum(weights, axis=-1)  9.77 us
    all_to_all x1, waiting for transfers between devices, shards(): lax.all_to_all(key_heads, 'inner', split_axis=1, concat_axis=0, tiled=True)  8.01 us
    all_to_all x1, waiting for transfers between devices, shards(): lax.all_to_all(value_heads, 'inner', split_axis=1, concat_axis=0, tiled=T...  7.37 us
  transfers between devices with their start and end apart: 7, of which 3 were waited for; matrix products, arithmetic and copies ran while one was open for 32% of the time, Pallas kernels for 0%

commit v1 on v0

--- a/solution.py
+++ b/solution.py
@@ -6,6 +6,18 @@
 QH = 32
 KVH = 8
 HD = 128
+
+
+def exchange_directly(x, axis, split, join):
+    ways, here = (lax.axis_size(axis), lax.axis_index(axis))
+    width = x.shape[split] // ways
+    turned = jnp.roll(x, -here * width, axis=split)
+    got = [lax.slice_in_dim(turned, 0, width, axis=split)]
+    for far in range(1, ways):
+        sent = lax.slice_in_dim(turned, far * width, (far + 1) * width, axis=split)
+        got.append(lax.ppermute(sent, axis, [(d, (d + far) % ways) for d in range(ways)]))
+    line = jnp.concatenate(got[::-1], axis=join)
+    return jnp.roll(line, (here + 1) * got[0].shape[join], axis=join)
 
 
 def shifted(block, axis, distance):
@@ -82,7 +94,7 @@
     peak, total, accum = state
     mixed = (accum / total[..., None]).astype(jnp.bfloat16)
     mixed = mixed.reshape(per_device, rows, HD).transpose(1, 0, 2)
-    back = lax.all_to_all(mixed, "inner", split_axis=0, concat_axis=1, tiled=True)
+    back = exchange_directly(mixed, "inner", 0, 1)
     return back.reshape(tokens, QH * HD)
 
 

time: 176 us -> 166 us (0.943)
  blocking collectives: 29 us -> 0 us
  waiting for transfers between devices: 29.9 us -> 50.5 us
  other arithmetic: 16.8 us -> 11.9 us
  starting transfers between devices: 25.3 us -> 29.4 us
    all_to_all x1 -> x0, blocking collectives: 29 us -> none  [shards(): lax.all_to_all(mixed, 'inner', split_axis=0, concat_axis=1, tiled=True)]
    ppermute x0 -> x7, waiting for transfers between devices: none -> 19.7 us  [exchange_directly(): lax.ppermute(sent, axis, [(d, (d + far) % ways) for d in range(ways)])]
    transpose x1, other arithmetic: 6.53 us -> 0.73 us  [shards(): mixed = mixed.reshape(per_device, rows, HD).transpose(1, 0, 2)]
    ppermute x0 -> x7, starting transfers between devices: none -> 4.16 us  [exchange_directly(): lax.ppermute(sent, axis, [(d, (d + far) % ways) for d in range(ways)])]
    unnamed x9 -> x26, local copies, waits for them, and re-layouts: 4.9 us -> 4.22 us
  transfers between devices with their start and end apart: 7 -> 14, of which waited for: 3 -> 8; matrix products, arithmetic and copies ran while one was open for 32% -> 34% of each run, Pallas kernels for 0% -> 0%
where the time goes in v1:
time: 166 us; the launch traced here: 164 us
  matrix products  61.1 us (37%)
  waiting for transfers between devices  50.5 us (30%)
  starting transfers between devices  29.4 us (18%)
  other arithmetic  11.9 us (7%)
  local copies, waits for them, and re-layouts  10.3 us (6%)
    dot_general x12, matrix products, one_block(): jnp.einsum('grqk,kgd->grqd', weights.astype(jnp.bfloat16), value_block, p...  34.6 us
    dot_general x12, matrix products, one_block(): jnp.einsum('qgrd,kgd->grqk', grouped, key_block, preferred_element_type=j...  26.6 us
    ppermute x7, waiting for transfers between devices, exchange_directly(): lax.ppermute(sent, axis, [(d, (d + far) % ways) for d in range(ways)])  19.7 us
    all_to_all x1, waiting for transfers between devices, shards(): lax.all_to_all(query_heads, 'inner', split_axis=1, concat_axis=0, tiled=T...  14.5 us
    ppermute x4, starting transfers between devices, shifted(): return lax.ppermute(block, axis, route)  11.9 us
    reduce_sum x12, other arithmetic, one_block(): total = total * factor + jnp.sum(weights, axis=-1)  9.77 us
    all_to_all x1, waiting for transfers between devices, shards(): lax.all_to_all(value_heads, 'inner', split_axis=1, concat_axis=0, tiled=T...  8.32 us
    all_to_all x1, waiting for transfers between devices, shards(): lax.all_to_all(key_heads, 'inner', split_axis=1, concat_axis=0, tiled=True)  8.01 us
  transfers between devices with their start and end apart: 14, of which 8 were waited for; matrix products, arithmetic and copies ran while one was open for 34% of the time, Pallas kernels for 0%

profile of v1, /device:TPU:0, one launch (start us, length us, event | category | flops | bytes accessed | tf_op | source)
XLA Modules:
  0.0 164.1 jit_solution(15049226792871771350)
XLA Ops:
  0.0 0.9 copy-done
  1.0 0.8 copy_bitcast_fusion.2
  1.7 6.4 %all-to-all-start = ((bf16[128,8,128]{2,0,1:T(8,128)(2,1)}), bf16[128,8,128]{2,0,1:T(8,128)(2,1)S(1)}, u32[]{:S(2)}, u32[]{:S(2)}) async-start(bf16[128,8,128]{2,0,1:T(8,128)(2,1)} %copy_bitcast_fusion.2), calls=%async_computation | async-start | bytes 524288 | tf_op jit(solution)/shard_map/all_to_all | solution.py:84
  8.1 1.7 %copy_bitcast_fusion.1 = bf16[128,8,128]{2,0,1:T(8,128)(2,1)} fusion(bf16[128,1024]{1,0:T(8,128)(2,1)} %param.11), kind=kLoop, calls=%fused_computation.86 | loop fusion | bytes 524288 | tf_op jit(solution)/shard_map/reshape;broadcast_in_dim;reshape | solution.py:81
  9.8 8.0 %all-to-all-done = bf16[128,8,128]{2,0,1:T(8,128)(2,1)S(1)} async-done(((bf16[128,8,128]{2,0,1:T(8,128)(2,1)}), bf16[128,8,128]{2,0,1:T(8,128)(2,1)S(1)}, u32[]{:S(2)}, u32[]{:S(2)}) %all-to-all-start) | async-done | bytes 262176 | tf_op jit(solution)/shard_map/all_to_all | solution.py:84
  17.8 3.4 %all-to-all-start.2 = ((bf16[128,8,128]{2,0,1:T(8,128)(2,1)}), bf16[128,8,128]{2,0,1:T(8,128)(2,1)S(1)}, u32[]{:S(2)}, u32[]{:S(2)}) async-start(bf16[128,8,128]{2,0,1:T(8,128)(2,1)} %copy_bitcast_fusion.1), calls=%async_computation.2 | async-start | bytes 524288 | tf_op jit(solution)/shard_map/all_to_all | solution.py:85
  21.2 1.3 copy.20
  22.5 8.3 %all-to-all-done.2 = bf16[128,8,128]{2,0,1:T(8,128)(2,1)S(1)} async-done(((bf16[128,8,128]{2,0,1:T(8,128)(2,1)}), bf16[128,8,128]{2,0,1:T(8,128)(2,1)S(1)}, u32[]{:S(2)}, u32[]{:S(2)}) %all-to-all-start.2) | async-done | bytes 262176 | tf_op jit(solution)/shard_map/all_to_all | solution.py:85
  31.5 3.6 %all-to-all-start.1 = ((bf16[128,32,128]{0,2,1:T(8,128)(2,1)}), bf16[128,32,128]{0,2,1:T(8,128)(2,1)S(1)}, u32[]{:S(2)}, u32[]{:S(2)}) async-start(bf16[128,32,128]{0,2,1:T(8,128)(2,1)} %bitcast.31), calls=%async_computation.1 | async-start | bytes 2097152 | tf_op jit(solution)/shard_map/all_to_all | solution.py:83
  35.2 4.1 %collective-permute-start = (bf16[1024,1,128]{2,0,1:T(8,128)(2,1)}, bf16[1024,1,128]{2,0,1:T(8,128)(2,1)}, u32[]{:S(2)}, u32[]{:S(2)}) collective-permute-start(bf16[1024,1,128]{2,0,1:T(8,128)(2,1)} %bitcast.262), channel_id=1, source_target_pairs={{0,8},{8,16},{16,24},{1,9},{9,17},{17,25},{2,10},{10,18},{18,26},{... | collective-permute-start | bytes 786440 | tf_op jit(solution)/shard_map/ppermute | solution.py:26
  39.3 1.3 collective-permute-start.2
  40.6 5.3 %collective-permute-start.1 = (bf16[1024,1,128]{2,0,1:T(8,128)(2,1)}, bf16[1024,1,128]{2,0,1:T(8,128)(2,1)}, u32[]{:S(2)}, u32[]{:S(2)}) collective-permute-start(bf16[1024,1,128]{2,0,1:T(8,128)(2,1)} %bitcast.265), channel_id=1, source_target_pairs={{0,8},{8,16},{16,24},{1,9},{9,17},{17,25},{2,10},{10,18},{18,26},{... | collective-permute-start | bytes 786440 | tf_op jit(solution)/shard_map/ppermute | solution.py:26
  45.8 1.3 collective-permute-start.3
  47.1 14.5 %all-to-all-done.1 = bf16[128,32,128]{0,2,1:T(8,128)(2,1)S(1)} async-done(((bf16[128,32,128]{0,2,1:T(8,128)(2,1)}), bf16[128,32,128]{0,2,1:T(8,128)(2,1)S(1)}, u32[]{:S(2)}, u32[]{:S(2)}) %all-to-all-start.1) | async-done | bytes 1048608 | tf_op jit(solution)/shard_map/all_to_all | solution.py:83
  61.6 1.0 copy-done.2
  62.6 1.6 copy.22
  64.2 31.1 %while.45 = (s32[]{:T(128)}, f32[1,4,1024]{2,1,0:T(4,128)S(1)}, f32[1,4,1024]{2,1,0:T(4,128)S(1)}, f32[1,4,1024,128]{3,2,1,0:T(8,128)S(1)}, bf16[4,256,1,128]{3,...) while((s32[]{:T(128)}, f32[1,4,1024]{2,1,0:T(4,128)S(1)}, ...), condition=%wide.region_3.4_spmd.clone, body=%wide.region_0.3_spmd.clone.sunk | while | flops 546856960 | bytes 34997380 | solution.py:59
  64.2 3.5 %bitcast_reduce_fusion.8 = (f32[4,1024]{1,0:T(4,128)S(1)}, f32[256,1024,4]{1,0,2:T(8,128)}) fusion(bf16[1024,1,4,128]{3,0,2,1:T(8,128)(2,1)S(1)} %get-tuple-element.416, bf16[4,256,1,128]{3,1,2,0:T(8,128)(2,1)} %get-tuple-element.415, s32[]{:T(128)} %get-tuple-element.402), kind=kOutput, calls=%fused_computation.55.clone.1 | convolution fusion | flops 270528512 | bytes 5325312 | tf_op jit(solution)/shard_map/while/body/eval_jaxpr/qgrd,kgd->grqk/dot_general | solution.py:42
  67.7 3.3 %bitcast_add_fusion.17 = f32[1,4,1024,128]{3,2,1,0:T(8,128)S(1)} fusion(f32[1,4,1024,128]{3,2,1,0:T(8,128)S(1)} %get-tuple-element.405, f32[256,1024,4]{1,0,2:T(8,128)} %get-tuple-element.391, f32[4,1024]{1,0:T(4,128)S(1)} %bitcast.254, f32[4,1024]{1,0:T(4,128)S(1)} %get-tuple-element.392, pred[]{:T(512)S(6)} %compare.5, ...), kind=kOutput, calls=%fused_computation.61.clone.1 | convolution fusion | flops 273154048 | bytes 8487425 | tf_op jit(solution)/shard_map/while/body/eval_jaxpr/grqk,kgd->grqd/dot_general | solution.py:50
  71.2 0.7 fusion.94
  72.0 3.5 %bitcast_reduce_fusion.8 = (f32[4,1024]{1,0:T(4,128)S(1)}, f32[256,1024,4]{1,0,2:T(8,128)}) fusion(bf16[1024,1,4,128]{3,0,2,1:T(8,128)(2,1)S(1)} %get-tuple-element.416, bf16[4,256,1,128]{3,1,2,0:T(8,128)(2,1)} %get-tuple-element.415, s32[]{:T(128)} %get-tuple-element.402), kind=kOutput, calls=%fused_computation.55.clone.1 | convolution fusion | flops 270528512 | bytes 5325312 | tf_op jit(solution)/shard_map/while/body/eval_jaxpr/qgrd,kgd->grqk/dot_general | solution.py:42
  75.5 3.3 %bitcast_add_fusion.17 = f32[1,4,1024,128]{3,2,1,0:T(8,128)S(1)} fusion(f32[1,4,1024,128]{3,2,1,0:T(8,128)S(1)} %get-tuple-element.405, f32[256,1024,4]{1,0,2:T(8,128)} %get-tuple-element.391, f32[4,1024]{1,0:T(4,128)S(1)} %bitcast.254, f32[4,1024]{1,0:T(4,128)S(1)} %get-tuple-element.392, pred[]{:T(512)S(6)} %compare.5, ...), kind=kOutput, calls=%fused_computation.61.clone.1 | convolution fusion | flops 273154048 | bytes 8487425 | tf_op jit(solution)/shard_map/while/body/eval_jaxpr/grqk,kgd->grqd/dot_general | solution.py:50
  79.0 0.7 fusion.94
  79.8 3.5 %bitcast_reduce_fusion.8 = (f32[4,1024]{1,0:T(4,128)S(1)}, f32[256,1024,4]{1,0,2:T(8,128)}) fusion(bf16[1024,1,4,128]{3,0,2,1:T(8,128)(2,1)S(1)} %get-tuple-element.416, bf16[4,256,1,128]{3,1,2,0:T(8,128)(2,1)} %get-tuple-element.415, s32[]{:T(128)} %get-tuple-element.402), kind=kOutput, calls=%fused_computation.55.clone.1 | convolution fusion | flops 270528512 | bytes 5325312 | tf_op jit(solution)/shard_map/while/body/eval_jaxpr/qgrd,kgd->grqk/dot_general | solution.py:42
  83.3 3.3 %bitcast_add_fusion.17 = f32[1,4,1024,128]{3,2,1,0:T(8,128)S(1)} fusion(f32[1,4,1024,128]{3,2,1,0:T(8,128)S(1)} %get-tuple-element.405, f32[256,1024,4]{1,0,2:T(8,128)} %get-tuple-element.391, f32[4,1024]{1,0:T(4,128)S(1)} %bitcast.254, f32[4,1024]{1,0:T(4,128)S(1)} %get-tuple-element.392, pred[]{:T(512)S(6)} %compare.5, ...), kind=kOutput, calls=%fused_computation.61.clone.1 | convolution fusion | flops 273154048 | bytes 8487425 | tf_op jit(solution)/shard_map/while/body/eval_jaxpr/grqk,kgd->grqd/dot_general | solution.py:50
  87.5 3.5 %bitcast_reduce_fusion.8 = (f32[4,1024]{1,0:T(4,128)S(1)}, f32[256,1024,4]{1,0,2:T(8,128)}) fusion(bf16[1024,1,4,128]{3,0,2,1:T(8,128)(2,1)S(1)} %get-tuple-element.416, bf16[4,256,1,128]{3,1,2,0:T(8,128)(2,1)} %get-tuple-element.415, s32[]{:T(128)} %get-tuple-element.402), kind=kOutput, calls=%fused_computation.55.clone.1 | convolution fusion | flops 270528512 | bytes 5325312 | tf_op jit(solution)/shard_map/while/body/eval_jaxpr/qgrd,kgd->grqk/dot_general | solution.py:42
  91.1 3.3 %bitcast_add_fusion.17 = f32[1,4,1024,128]{3,2,1,0:T(8,128)S(1)} fusion(f32[1,4,1024,128]{3,2,1,0:T(8,128)S(1)} %get-tuple-element.405, f32[256,1024,4]{1,0,2:T(8,128)} %get-tuple-element.391, f32[4,1024]{1,0:T(4,128)S(1)} %bitcast.254, f32[4,1024]{1,0:T(4,128)S(1)} %get-tuple-element.392, pred[]{:T(512)S(6)} %compare.5, ...), kind=kOutput, calls=%fused_computation.61.clone.1 | convolution fusion | flops 273154048 | bytes 8487425 | tf_op jit(solution)/shard_map/while/body/eval_jaxpr/grqk,kgd->grqd/dot_general | solution.py:50
  94.5 0.7 fusion.94
  95.3 20.8 %while.43 = (s32[]{:T(128)}, f32[1,4,1024]{2,1,0:T(4,128)S(1)}, f32[1,4,1024]{2,1,0:T(4,128)S(1)}, f32[1,4,1024,128]{3,2,1,0:T(8,128)S(1)}, pred[]{:T(512)}, /*i...) while((s32[]{:T(128)}, f32[1,4,1024]{2,1,0:T(4,128)S(1)}, ...), condition=%wide.region_7.8_spmd, body=%wide.region_4.7_spmd.sunk | while | flops 549466112 | bytes 18221148 | solution.py:59
  95.3 1.6 bitcast_reduce_fusion.6
  96.9 2.7 %bitcast_add_fusion.13 = f32[1,4,1024,128]{3,2,1,0:T(8,128)S(1)} fusion(f32[1,4,1024,128]{3,2,1,0:T(8,128)S(1)} %get-tuple-element.432, f32[256,1024,4]{1,0,2:T(8,128)S(1)} %get-tuple-element.368, f32[4,1024]{1,0:T(4,128)S(1)} %bitcast.256, pred[]{:T(512)} %get-tuple-element.442, f32[4,1024]{1,0:T(4,128)S(1)} %get-tuple-element.369, ...), kind=kOutput, calls=%fused_computation.8.clone.1 | convolution fusion | flops 273678336 | bytes 8487936 | tf_op jit(solution)/shard_map/while/body/eval_jaxpr/grqk,kgd->grqd/dot_general | solution.py:50
  99.6 0.9 fusion.86
  100.5 1.6 bitcast_reduce_fusion.6
  102.1 2.7 %bitcast_add_fusion.13 = f32[1,4,1024,128]{3,2,1,0:T(8,128)S(1)} fusion(f32[1,4,1024,128]{3,2,1,0:T(8,128)S(1)} %get-tuple-element.432, f32[256,1024,4]{1,0,2:T(8,128)S(1)} %get-tuple-element.368, f32[4,1024]{1,0:T(4,128)S(1)} %bitcast.256, pred[]{:T(512)} %get-tuple-element.442, f32[4,1024]{1,0:T(4,128)S(1)} %get-tuple-element.369, ...), kind=kOutput, calls=%fused_computation.8.clone.1 | convolution fusion | flops 273678336 | bytes 8487936 | tf_op jit(solution)/shard_map/while/body/eval_jaxpr/grqk,kgd->grqd/dot_general | solution.py:50
  104.8 0.9 fusion.86
  105.7 1.6 bitcast_reduce_fusion.6
  107.3 2.7 %bitcast_add_fusion.13 = f32[1,4,1024,128]{3,2,1,0:T(8,128)S(1)} fusion(f32[1,4,1024,128]{3,2,1,0:T(8,128)S(1)} %get-tuple-element.432, f32[256,1024,4]{1,0,2:T(8,128)S(1)} %get-tuple-element.368, f32[4,1024]{1,0:T(4,128)S(1)} %bitcast.256, pred[]{:T(512)} %get-tuple-element.442, f32[4,1024]{1,0:T(4,128)S(1)} %get-tuple-element.369, ...), kind=kOutput, calls=%fused_computation.8.clone.1 | convolution fusion | flops 273678336 | bytes 8487936 | tf_op jit(solution)/shard_map/while/body/eval_jaxpr/grqk,kgd->grqd/dot_general | solution.py:50
  110.0 0.9 fusion.86
  110.9 1.6 bitcast_reduce_fusion.6
  112.5 2.7 %bitcast_add_fusion.13 = f32[1,4,1024,128]{3,2,1,0:T(8,128)S(1)} fusion(f32[1,4,1024,128]{3,2,1,0:T(8,128)S(1)} %get-tuple-element.432, f32[256,1024,4]{1,0,2:T(8,128)S(1)} %get-tuple-element.368, f32[4,1024]{1,0:T(4,128)S(1)} %bitcast.256, pred[]{:T(512)} %get-tuple-element.442, f32[4,1024]{1,0:T(4,128)S(1)} %get-tuple-element.369, ...), kind=kOutput, calls=%fused_computation.8.clone.1 | convolution fusion | flops 273678336 | bytes 8487936 | tf_op jit(solution)/shard_map/while/body/eval_jaxpr/grqk,kgd->grqd/dot_general | solution.py:50
  115.2 0.9 fusion.86
  116.2 20.8 %while.44 = (s32[]{:T(128)}, f32[1,4,1024]{2,1,0:T(4,128)S(1)}, f32[1,4,1024]{2,1,0:T(4,128)S(1)}, f32[1,4,1024,128]{3,2,1,0:T(8,128)S(1)}, pred[]{:T(512)}, /*i...) while((s32[]{:T(128)}, f32[1,4,1024]{2,1,0:T(4,128)S(1)}, ...), condition=%wide.region_11.12_spmd, body=%wide.region_8.11_spmd.sunk | while | flops 549466112 | bytes 18221148 | solution.py:59
  116.2 1.6 bitcast_reduce_fusion.7
  117.8 2.7 %bitcast_add_fusion.15 = f32[1,4,1024,128]{3,2,1,0:T(8,128)S(1)} fusion(f32[1,4,1024,128]{3,2,1,0:T(8,128)S(1)} %get-tuple-element.459, f32[256,1024,4]{1,0,2:T(8,128)S(1)} %get-tuple-element.380, f32[4,1024]{1,0:T(4,128)S(1)} %bitcast.258, pred[]{:T(512)} %get-tuple-element.469, f32[4,1024]{1,0:T(4,128)S(1)} %get-tuple-element.381, ...), kind=kOutput, calls=%fused_computation.35.clone.1 | convolution fusion | flops 273678336 | bytes 8487936 | tf_op jit(solution)/shard_map/while/body/eval_jaxpr/grqk,kgd->grqd/dot_general | solution.py:50
  120.4 0.9 fusion.90
  121.4 1.6 bitcast_reduce_fusion.7
  123.0 2.7 %bitcast_add_fusion.15 = f32[1,4,1024,128]{3,2,1,0:T(8,128)S(1)} fusion(f32[1,4,1024,128]{3,2,1,0:T(8,128)S(1)} %get-tuple-element.459, f32[256,1024,4]{1,0,2:T(8,128)S(1)} %get-tuple-element.380, f32[4,1024]{1,0:T(4,128)S(1)} %bitcast.258, pred[]{:T(512)} %get-tuple-element.469, f32[4,1024]{1,0:T(4,128)S(1)} %get-tuple-element.381, ...), kind=kOutput, calls=%fused_computation.35.clone.1 | convolution fusion | flops 273678336 | bytes 8487936 | tf_op jit(solution)/shard_map/while/body/eval_jaxpr/grqk,kgd->grqd/dot_general | solution.py:50
  125.7 0.9 fusion.90
  126.6 1.6 bitcast_reduce_fusion.7
  128.2 2.7 %bitcast_add_fusion.15 = f32[1,4,1024,128]{3,2,1,0:T(8,128)S(1)} fusion(f32[1,4,1024,128]{3,2,1,0:T(8,128)S(1)} %get-tuple-element.459, f32[256,1024,4]{1,0,2:T(8,128)S(1)} %get-tuple-element.380, f32[4,1024]{1,0:T(4,128)S(1)} %bitcast.258, pred[]{:T(512)} %get-tuple-element.469, f32[4,1024]{1,0:T(4,128)S(1)} %get-tuple-element.381, ...), kind=kOutput, calls=%fused_computation.35.clone.1 | convolution fusion | flops 273678336 | bytes 8487936 | tf_op jit(solution)/shard_map/while/body/eval_jaxpr/grqk,kgd->grqd/dot_general | solution.py:50
  130.9 0.9 fusion.90
  131.8 1.6 bitcast_reduce_fusion.7
  133.4 2.7 %bitcast_add_fusion.15 = f32[1,4,1024,128]{3,2,1,0:T(8,128)S(1)} fusion(f32[1,4,1024,128]{3,2,1,0:T(8,128)S(1)} %get-tuple-element.459, f32[256,1024,4]{1,0,2:T(8,128)S(1)} %get-tuple-element.380, f32[4,1024]{1,0:T(4,128)S(1)} %bitcast.258, pred[]{:T(512)} %get-tuple-element.469, f32[4,1024]{1,0:T(4,128)S(1)} %get-tuple-element.381, ...), kind=kOutput, calls=%fused_computation.35.clone.1 | convolution fusion | flops 273678336 | bytes 8487936 | tf_op jit(solution)/shard_map/while/body/eval_jaxpr/grqk,kgd->grqd/dot_general | solution.py:50
  136.1 0.9 fusion.90
  137.0 0.7 fusion.67
  137.7 0.9 fusion.66
  138.7 1.0 collective-permute-start.4
  140.1 2.7 %collective-permute-start.7 = (bf16[128,4,128]{2,0,1:T(8,128)(2,1)S(1)}, bf16[128,4,128]{2,0,1:T(8,128)(2,1)S(1)}, u32[]{:S(2)}, u32[]{:S(2)}) collective-permute-start(bf16[128,4,128]{2,0,1:T(8,128)(2,1)S(1)} %get-tuple-element.224), channel_id=1, source_target_pairs={{0,4},{1,5},{2,6},{3,7},{4,0},{5,1},{6,2},{7,3},{8,12},{9,13},{10,... | collective-permute-start | bytes 393224 | tf_op jit(solution)/shard_map/ppermute | solution.py:18
  142.9 0.8 collective-permute-done.4
  143.7 4.4 %collective-permute-done.5 = bf16[128,4,128]{2,0,1:T(8,128)(2,1)S(1)} collective-permute-done((bf16[128,4,128]{2,0,1:T(8,128)(2,1)S(1)}, bf16[128,4,128]{2,0,1:T(8,128)(2,1)S(1)}, u32[]{:S(2)}, u32[]{:S(2)}) %collective-permute-start.5) | collective-permute-done | bytes 131104 | tf_op jit(solution)/shard_map/ppermute | solution.py:18
  148.1 1.2 collective-permute-done.6
  149.3 12.1 %collective-permute-done.7 = bf16[128,4,128]{2,0,1:T(8,128)(2,1)S(1)} collective-permute-done((bf16[128,4,128]{2,0,1:T(8,128)(2,1)S(1)}, bf16[128,4,128]{2,0,1:T(8,128)(2,1)S(1)}, u32[]{:S(2)}, u32[]{:S(2)}) %collective-permute-start.7) | collective-permute-done | bytes 131104 | tf_op jit(solution)/shard_map/ppermute | solution.py:18
  161.4 1.2 collective-permute-done.8
  163.0 1.1 copy_bitcast_fusion
  (84 shorter events, 3.5 us)
Async XLA Ops:
  0.0 1.0 copy-start
  1.0 20.2 %copy-start.5 = (bf16[128,4096]{1,0:T(8,128)(2,1)S(1)}, bf16[128,4096]{1,0:T(8,128)(2,1)}, u32[]{:S(2)}) copy-start(bf16[128,4096]{1,0:T(8,128)(2,1)} %param.9) | copy-start | bytes 3145732
  1.7 16.1 %all-to-all-start = ((bf16[128,8,128]{2,0,1:T(8,128)(2,1)}), bf16[128,8,128]{2,0,1:T(8,128)(2,1)S(1)}, u32[]{:S(2)}, u32[]{:S(2)}) async-start(bf16[128,8,128]{2,0,1:T(8,128)(2,1)} %copy_bitcast_fusion.2), calls=%async_computation | async-start | bytes 524288 | tf_op jit(solution)/shard_map/all_to_all | solution.py:84
  17.8 13.1 %copy-start.3 = (bf16[128,8,128]{2,0,1:T(8,128)(2,1)}, bf16[128,8,128]{2,0,1:T(8,128)(2,1)S(1)}, u32[]{:S(2)}) copy-start(bf16[128,8,128]{2,0,1:T(8,128)(2,1)S(1)} %all-to-all-done) | copy-start | bytes 786436
  17.8 13.1 %all-to-all-start.2 = ((bf16[128,8,128]{2,0,1:T(8,128)(2,1)}), bf16[128,8,128]{2,0,1:T(8,128)(2,1)S(1)}, u32[]{:S(2)}, u32[]{:S(2)}) async-start(bf16[128,8,128]{2,0,1:T(8,128)(2,1)} %copy_bitcast_fusion.1), calls=%async_computation.2 | async-start | bytes 524288 | tf_op jit(solution)/shard_map/all_to_all | solution.py:85
  30.8 0.7 copy-start.4
  31.5 30.1 %all-to-all-start.1 = ((bf16[128,32,128]{0,2,1:T(8,128)(2,1)}), bf16[128,32,128]{0,2,1:T(8,128)(2,1)S(1)}, u32[]{:S(2)}, u32[]{:S(2)}) async-start(bf16[128,32,128]{0,2,1:T(8,128)(2,1)} %bitcast.31), calls=%async_computation.1 | async-start | bytes 2097152 | tf_op jit(solution)/shard_map/all_to_all | solution.py:83
  35.2 60.1 %collective-permute-start = (bf16[1024,1,128]{2,0,1:T(8,128)(2,1)}, bf16[1024,1,128]{2,0,1:T(8,128)(2,1)}, u32[]{:S(2)}, u32[]{:S(2)}) collective-permute-start(bf16[1024,1,128]{2,0,1:T(8,128)(2,1)} %bitcast.262), channel_id=1, source_target_pairs={{0,8},{8,16},{16,24},{1,9},{9,17},{17,25},{2,10},{10,18},{18,26},{... | collective-permute-start | bytes 786440 | tf_op jit(solution)/shard_map/ppermute | solution.py:26
  39.3 76.8 %collective-permute-start.2 = (bf16[1024,1,128]{2,0,1:T(8,128)(2,1)}, bf16[1024,1,128]{2,0,1:T(8,128)(2,1)}, u32[]{:S(2)}, u32[]{:S(2)}) collective-permute-start(bf16[1024,1,128]{2,0,1:T(8,128)(2,1)} %bitcast.263), channel_id=1, source_target_pairs={{8,0},{16,8},{24,16},{9,1},{17,9},{25,17},{10,2},{18,10},{26,18},{... | collective-permute-start | bytes 786440 | tf_op jit(solution)/shard_map/ppermute | solution.py:26
  40.6 54.7 %collective-permute-start.1 = (bf16[1024,1,128]{2,0,1:T(8,128)(2,1)}, bf16[1024,1,128]{2,0,1:T(8,128)(2,1)}, u32[]{:S(2)}, u32[]{:S(2)}) collective-permute-start(bf16[1024,1,128]{2,0,1:T(8,128)(2,1)} %bitcast.265), channel_id=1, source_target_pairs={{0,8},{8,16},{16,24},{1,9},{9,17},{17,25},{2,10},{10,18},{18,26},{... | collective-permute-start | bytes 786440 | tf_op jit(solution)/shard_map/ppermute | solution.py:26
  45.8 70.3 %collective-permute-start.3 = (bf16[1024,1,128]{2,0,1:T(8,128)(2,1)}, bf16[1024,1,128]{2,0,1:T(8,128)(2,1)}, u32[]{:S(2)}, u32[]{:S(2)}) collective-permute-start(bf16[1024,1,128]{2,0,1:T(8,128)(2,1)} %bitcast.266), channel_id=1, source_target_pairs={{8,0},{16,8},{24,16},{9,1},{17,9},{25,17},{10,2},{18,10},{26,18},{... | collective-permute-start | bytes 786440 | tf_op jit(solution)/shard_map/ppermute | solution.py:26
  61.6 1.0 copy-start.2
  67.7 3.5 %copy-start.1 = (f32[256,1024,4]{1,0,2:T(8,128)S(1)}, f32[256,1024,4]{1,0,2:T(8,128)}, u32[]{:S(2)}) copy-start(f32[256,1024,4]{1,0,2:T(8,128)} %get-tuple-element.391) | copy-start | bytes 12582916 | tf_op jit(solution)/shard_map/while
  75.5 3.5 %copy-start.1 = (f32[256,1024,4]{1,0,2:T(8,128)S(1)}, f32[256,1024,4]{1,0,2:T(8,128)}, u32[]{:S(2)}) copy-start(f32[256,1024,4]{1,0,2:T(8,128)} %get-tuple-element.391) | copy-start | bytes 12582916 | tf_op jit(solution)/shard_map/while
  83.3 3.5 %copy-start.1 = (f32[256,1024,4]{1,0,2:T(8,128)S(1)}, f32[256,1024,4]{1,0,2:T(8,128)}, u32[]{:S(2)}) copy-start(f32[256,1024,4]{1,0,2:T(8,128)} %get-tuple-element.391) | copy-start | bytes 12582916 | tf_op jit(solution)/shard_map/while
  91.1 3.5 %copy-start.1 = (f32[256,1024,4]{1,0,2:T(8,128)S(1)}, f32[256,1024,4]{1,0,2:T(8,128)}, u32[]{:S(2)}) copy-start(f32[256,1024,4]{1,0,2:T(8,128)} %get-tuple-element.391) | copy-start | bytes 12582916 | tf_op jit(solution)/shard_map/while
  138.7 4.9 %collective-permute-start.4 = (bf16[128,4,128]{2,0,1:T(8,128)(2,1)S(1)}, bf16[128,4,128]{2,0,1:T(8,128)(2,1)S(1)}, u32[]{:S(2)}, u32[]{:S(2)}) collective-permute-start(bf16[128,4,128]{2,0,1:T(8,128)(2,1)S(1)} %get-tuple-element.227), channel_id=1, source_target_pairs={{0,7},{1,0},{2,1},{3,2},{4,3},{5,4},{6,5},{7,6},{8,15},{9,8},{10,9... | collective-permute-start | bytes 393224 | tf_op jit(solution)/shard_map/ppermute | solution.py:18
  139.7 8.4 %collective-permute-start.5 = (bf16[128,4,128]{2,0,1:T(8,128)(2,1)S(1)}, bf16[128,4,128]{2,0,1:T(8,128)(2,1)S(1)}, u32[]{:S(2)}, u32[]{:S(2)}) collective-permute-start(bf16[128,4,128]{2,0,1:T(8,128)(2,1)S(1)} %get-tuple-element.226), channel_id=1, source_target_pairs={{0,6},{1,7},{2,0},{3,1},{4,2},{5,3},{6,4},{7,5},{8,14},{9,15},{10,... | collective-permute-start | bytes 393224 | tf_op jit(solution)/shard_map/ppermute | solution.py:18
  140.1 9.2 %collective-permute-start.6 = (bf16[128,4,128]{2,0,1:T(8,128)(2,1)S(1)}, bf16[128,4,128]{2,0,1:T(8,128)(2,1)S(1)}, u32[]{:S(2)}, u32[]{:S(2)}) collective-permute-start(bf16[128,4,128]{2,0,1:T(8,128)(2,1)S(1)} %get-tuple-element.225), channel_id=1, source_target_pairs={{0,5},{1,6},{2,7},{3,0},{4,1},{5,2},{6,3},{7,4},{8,13},{9,14},{10,... | collective-permute-start | bytes 393224 | tf_op jit(solution)/shard_map/ppermute | solution.py:18
  140.1 21.3 %collective-permute-start.7 = (bf16[128,4,128]{2,0,1:T(8,128)(2,1)S(1)}, bf16[128,4,128]{2,0,1:T(8,128)(2,1)S(1)}, u32[]{:S(2)}, u32[]{:S(2)}) collective-permute-start(bf16[128,4,128]{2,0,1:T(8,128)(2,1)S(1)} %get-tuple-element.224), channel_id=1, source_target_pairs={{0,4},{1,5},{2,6},{3,7},{4,0},{5,1},{6,2},{7,3},{8,12},{9,13},{10,... | collective-permute-start | bytes 393224 | tf_op jit(solution)/shard_map/ppermute | solution.py:18
  142.8 19.8 %collective-permute-start.8 = (bf16[128,4,128]{2,0,1:T(8,128)(2,1)S(1)}, bf16[128,4,128]{2,0,1:T(8,128)(2,1)S(1)}, u32[]{:S(2)}, u32[]{:S(2)}) collective-permute-start(bf16[128,4,128]{2,0,1:T(8,128)(2,1)S(1)} %get-tuple-element.223), channel_id=1, source_target_pairs={{0,3},{1,4},{2,5},{3,6},{4,7},{5,0},{6,1},{7,2},{8,11},{9,12},{10,... | collective-permute-start | bytes 393224 | tf_op jit(solution)/shard_map/ppermute | solution.py:18
  143.6 19.0 %collective-permute-start.9 = (bf16[128,4,128]{2,0,1:T(8,128)(2,1)S(1)}, bf16[128,4,128]{2,0,1:T(8,128)(2,1)S(1)}, u32[]{:S(2)}, u32[]{:S(2)}) collective-permute-start(bf16[128,4,128]{2,0,1:T(8,128)(2,1)S(1)} %get-tuple-element.222), channel_id=1, source_target_pairs={{0,2},{1,3},{2,4},{3,5},{4,6},{5,7},{6,0},{7,1},{8,10},{9,11},{10,... | collective-permute-start | bytes 393224 | tf_op jit(solution)/shard_map/ppermute | solution.py:18
  148.1 14.6 %collective-permute-start.10 = (bf16[128,4,128]{2,0,1:T(8,128)(2,1)S(1)}, bf16[128,4,128]{2,0,1:T(8,128)(2,1)S(1)}, u32[]{:S(2)}, u32[]{:S(2)}) collective-permute-start(bf16[128,4,128]{2,0,1:T(8,128)(2,1)S(1)} %get-tuple-element.221), channel_id=1, source_target_pairs={{0,1},{1,2},{2,3},{3,4},{4,5},{5,6},{6,7},{7,0},{8,9},{9,10},{10,1... | collective-permute-start | bytes 393224 | tf_op jit(solution)/shard_map/ppermute | solution.py:18
